TPU v7x, 32 devices: a whole 2x2x4 slice. The times are simulated.
32 devices in a mesh: seg: 8 (over y, x, core), pos: 4 (over z).
Axes of the slice: x: 2, y: 2, z: 4, core: 2. Of those that a mesh axis runs over, the one named last changes fastest.
Arguments:
- query_heads: bfloat16 [32, 12, 128, 128], P('seg', None, 'pos'), may hold values from -32 to 32
- key_heads: bfloat16 [32, 12, 128, 128], P('seg', None, 'pos'), may hold values from -32 to 32
- value_heads: bfloat16 [32, 12, 128, 128], P('seg', None, 'pos'), may hold values from -6 to 6
- out_grad: bfloat16 [32, 12, 128, 128], P('seg', None, 'pos'), may hold values from -6 to 6
- clip_lengths: int32 [8], replicated, may hold values from 1 to 8, 32 in all
- clip_resolution: int32 [8], replicated, may hold values from 32 to 128
- clip_window: int32 [8], replicated, may hold values from 1 to 2
Outputs:
- grad_query: bfloat16 [32, 12, 128, 128], P('seg', None, 'pos')
- grad_key: bfloat16 [32, 12, 128, 128], P('seg', None, 'pos')
- grad_value: bfloat16 [32, 12, 128, 128], P('seg', None, 'pos')
All inputs are finite; a program needn't handle non-finite values.
Results may differ from a plain program's by a relative error of at most 0.025.
Values may be sent and summed in bfloat16 or wider, within the bound.
A program may use at most 64 MiB of HBM per device.

v0:
```python
import functools
import math

import jax
import jax.numpy as jnp
from jax import lax
from jax.experimental import pallas as pl
from jax.experimental.pallas import tpu as pltpu
from jax.sharding import PartitionSpec as P

WMAX = 2
MESH = pl.DeviceIdType.MESH
PARTS = 1


def matmul(left, right, dims):
    return lax.dot_general(left, right, (dims, ((), ())), preferred_element_type=jnp.float32)


def kernel(
    n,
    segs,
    chunk,
    q_ref,
    k_ref,
    v_ref,
    g_ref,
    len_ref,
    res_ref,
    win_ref,
    oq_ref,
    ok_ref,
    ov_ref,
    recv,
    back,
    saved,
    slopes,
    tqg,
    ekv,
    edge,
    redge,
    own,
    fwd_s,
    fwd_r,
    back_s,
    back_r,
    halo_s,
    halo_r,
    ret_s,
    ret_r,
    self_s,
    time_s,
):
    frames, heads, rows, width = q_ref.shape
    half = heads // 2
    items = frames * half // n
    pieces = items // chunk
    positions = n * rows
    inv_root = 1.0 / math.sqrt(width)
    ins = (q_ref, k_ref, v_ref, g_ref)
    outs = (oq_ref, ok_ref, ov_ref)
    seg = lax.axis_index("seg")
    pos = lax.axis_index("pos")
    right = lax.rem(seg + 1, segs)
    left = lax.rem(seg + segs - 1, segs)
    steps = sorted(range(1, n), key=lambda r: abs(r - n // 2))

    def rows_of(p):
        return pl.ds(pl.multiple_of(p * rows, rows), rows)

    def item_block(ref, owner, piece):
        first = owner * items + piece * chunk
        return ref.at[lax.div(first, half), pl.ds(lax.rem(first, half), chunk)]

    def fwd(a, piece, dest, source):
        return pltpu.make_async_remote_copy(
            src_ref=item_block(ins[a], dest, piece),
            dst_ref=recv.at[a, pl.ds(piece * chunk, chunk), rows_of(source)],
            send_sem=fwd_s.at[a, piece, dest],
            recv_sem=fwd_r.at[a, piece, source],
            device_id=(seg, dest),
            device_id_type=MESH,
        )

    def backward(a, piece, dest, source):
        return pltpu.make_async_remote_copy(
            src_ref=back.at[a, pl.ds(piece * chunk, chunk), rows_of(dest)],
            dst_ref=item_block(outs[a], source, piece),
            send_sem=back_s.at[a, piece, dest],
            recv_sem=back_r.at[a, piece, source],
            device_id=(seg, dest),
            device_id_type=MESH,
        )

    def self_in(a, piece):
        return pltpu.make_async_copy(
            item_block(ins[a], pos, piece),
            recv.at[a, pl.ds(piece * chunk, chunk), rows_of(pos)],
            self_s.at[a, piece],
        )

    def self_out(a, piece):
        return pltpu.make_async_copy(
            back.at[a, pl.ds(piece * chunk, chunk), rows_of(pos)],
            item_block(outs[a], pos, piece),
            self_s.at[4 + a, piece],
        )

    def time_half(ref, first, count):
        return ref.at[pl.ds(first, count), pl.ds(half, half)]

    def halo(way, a):
        source = (k_ref, v_ref)[a]
        if way == 0:
            src, dst, dest = time_half(source, frames - WMAX, WMAX), 0, right
        else:
            src, dst, dest = time_half(source, 0, WMAX), frames + WMAX, left
        return pltpu.make_async_remote_copy(
            src_ref=src,
            dst_ref=ekv.at[a, pl.ds(dst, WMAX)],
            send_sem=halo_s.at[way, a],
            recv_sem=halo_r.at[way, a],
            device_id=(dest, pos),
            device_id_type=MESH,
        )

    def give(way):
        return pltpu.make_async_remote_copy(
            src_ref=edge.at[way],
            dst_ref=redge.at[way],
            send_sem=ret_s.at[way],
            recv_sem=ret_r.at[way],
            device_id=((left, right)[way], pos),
            device_id_type=MESH,
        )

    time_in = [
        pltpu.make_async_copy(time_half(q_ref, 0, frames), tqg.at[0], time_s.at[0]),
        pltpu.make_async_copy(time_half(g_ref, 0, frames), tqg.at[1], time_s.at[1]),
        pltpu.make_async_copy(
            time_half(k_ref, 0, frames), ekv.at[0, pl.ds(WMAX, frames)], time_s.at[2]
        ),
        pltpu.make_async_copy(
            time_half(v_ref, 0, frames), ekv.at[1, pl.ds(WMAX, frames)], time_s.at[3]
        ),
    ]

    barrier = pltpu.get_barrier_semaphore()
    for r in steps:
        pl.semaphore_signal(
            barrier, inc=1, device_id=(seg, lax.rem(pos + r, n)), device_id_type=MESH
        )
    for near in (left, right):
        pl.semaphore_signal(barrier, inc=1, device_id=(near, pos), device_id_type=MESH)
    for copy in time_in:
        copy.start()
    for piece in range(pieces):
        for a in range(4):
            self_in(a, piece).start()
    pl.semaphore_wait(barrier, n + 1)

    for piece in range(pieces):
        for a in (0, 1, 3, 2):
            for r in steps:
                fwd(a, piece, lax.rem(pos + r, n), pos).start()
        if piece == 0:
            for way in range(2):
                for a in range(2):
                    halo(way, a).start()

    ext = frames + 2 * WMAX
    base = seg * frames
    zero = jnp.int32(0)

    def clip_step(c, carry):
        start, owners, live, wins = carry
        end = start + len_ref[c]
        owners = tuple(
            o + jnp.where(end <= base + (x - WMAX), 1, 0) for x, o in enumerate(owners)
        )
        inside = [(start <= base + x) & (base + x < end) for x in range(frames)]
        live = tuple(jnp.where(i, res_ref[c], o) for i, o in zip(inside, live))
        wins = tuple(jnp.where(i, win_ref[c], o) for i, o in zip(inside, wins))
        return end, owners, live, wins

    _, owners, live, wins = lax.fori_loop(
        0, len_ref.shape[0], clip_step, (zero, (zero,) * ext, (zero,) * frames, (zero,) * frames)
    )
    owners = [jnp.where(base + (x - WMAX) < 0, -1, o) for x, o in enumerate(owners)]
    bias = [
        [
            jnp.where(
                (owners[i + o] == owners[i + WMAX]) & (wins[i] >= abs(o - WMAX)), 0.0, -jnp.inf
            ).astype(jnp.float32)
            for o in range(2 * WMAX + 1)
        ]
        for i in range(frames)
    ]

    for copy in time_in:
        copy.wait()
    for way in range(2):
        for a in range(2):
            halo(way, a).wait_recv()

    def time_head(h, carry):
        row = lax.broadcasted_iota(jnp.int32, (rows, 1), 0) + pos * rows
        keys = [ekv[0, j, h].astype(jnp.float32) for j in range(ext)]
        values = [ekv[1, j, h].astype(jnp.float32) for j in range(ext)]
        key_sum = [None] * ext
        value_sum = [None] * ext
        for i in range(frames):
            query = tqg[0, i, h].astype(jnp.float32)
            grad = tqg[1, i, h].astype(jnp.float32)
            offsets = range(2 * WMAX + 1)
            scores = [
                jnp.sum(query * keys[i + o], axis=1, keepdims=True) * inv_root + bias[i][o]
                for o in offsets
            ]
            dweights = [jnp.sum(grad * values[i + o], axis=1, keepdims=True) for o in offsets]
            top = functools.reduce(jnp.maximum, scores)
            powers = [jnp.exp(s - top) for s in scores]
            scale = jnp.where(row < live[i], 1.0 / sum(powers[1:], powers[0]), 0.0)
            weights = [p * scale for p in powers]
            low = [w.astype(jnp.bfloat16).astype(jnp.float32) for w in weights]
            dots = [w * d for w, d in zip(low, dweights)]
            row_dot = sum(dots[1:], dots[0])
            dscores = [
                (w * (d - row_dot)).astype(jnp.bfloat16).astype(jnp.float32)
                for w, d in zip(weights, dweights)
            ]
            terms = [dscores[o] * keys[i + o] for o in offsets]
            oq_ref[i, half + h] = (sum(terms[1:], terms[0]) * inv_root).astype(jnp.bfloat16)
            for o in offsets:
                j = i + o
                key_term = dscores[o] * query
                value_term = low[o] * grad
                key_sum[j] = key_term if key_sum[j] is None else key_sum[j] + key_term
                value_sum[j] = value_term if value_sum[j] is None else value_sum[j] + value_term
        for a, sums in enumerate((key_sum, value_sum)):
            factor = inv_root if a == 0 else 1.0
            for j in range(WMAX):
                edge[0, a, j, h] = (sums[j] * factor).astype(jnp.bfloat16)
                edge[1, a, j, h] = (sums[frames + WMAX + j] * factor).astype(jnp.bfloat16)
            for i in range(frames):
                own[a, i, h] = sums[WMAX + i] * factor
        return carry

    lax.fori_loop(0, half, time_head, 0)
    for way in range(2):
        give(way).start()

    def arrived(a, piece):
        self_in(a, piece).wait()
        for r in steps:
            source = lax.rem(pos + r, n)
            fwd(a, piece, source, source).wait_recv()

    def send(a, piece):
        for r in steps:
            backward(a, piece, lax.rem(pos + r, n), pos).start()
        self_out(a, piece).start()

    for piece in range(pieces):
        span = range(piece * chunk, (piece + 1) * chunk)
        arrived(0, piece)
        arrived(1, piece)
        for t in span:
            frame = lax.div(pos * items + t, half)
            limit = sum(
                (jnp.where(frame == i, live[i], 0) for i in range(1, frames)),
                jnp.where(frame == 0, live[0], 0),
            )
            row = lax.broadcasted_iota(jnp.int32, (positions, 1), 0)
            col = lax.broadcasted_iota(jnp.int32, (1, positions), 1)
            scores = matmul(recv[0, t], recv[1, t], ((1,), (1,))) * inv_root
            scores = jnp.where(col < limit, scores, -jnp.inf)
            powers = jnp.exp(scores - jnp.max(scores, axis=1, keepdims=True))
            total = jnp.sum(powers, axis=1, keepdims=True)
            saved[t] = powers * jnp.where(row < limit, 1.0 / total, 0.0)
        arrived(3, piece)
        for t in span:
            low = saved[t].astype(jnp.bfloat16)
            back[2, t] = matmul(low, recv[3, t], ((0,), (0,))).astype(jnp.bfloat16)
        send(2, piece)
        arrived(2, piece)
        for t in span:
            weights = saved[t]
            low = weights.astype(jnp.bfloat16).astype(jnp.float32)
            dweights = matmul(recv[3, t], recv[2, t], ((1,), (1,)))
            row_dot = jnp.sum(low * dweights, axis=1, keepdims=True)
            dscores = (weights * (dweights - row_dot)).astype(jnp.bfloat16)
            slopes[t] = dscores
            query_part = matmul(dscores, recv[1, t], ((1,), (0,))) * inv_root
            back[0, t] = query_part.astype(jnp.bfloat16)
        send(0, piece)
        for t in span:
            key_part = matmul(slopes[t], recv[0, t], ((0,), (0,))) * inv_root
            back[1, t] = key_part.astype(jnp.bfloat16)
        send(1, piece)

    for way in range(2):
        give(way).wait_recv()

    def time_close(h, carry):
        for a in range(2):
            for i in range(frames):
                total = own[a, i, h]
                if i < WMAX:
                    total = total + redge[1, a, i, h].astype(jnp.float32)
                if i >= frames - WMAX:
                    total = total + redge[0, a, i - (frames - WMAX), h].astype(jnp.float32)
                outs[1 + a][i, half + h] = total.astype(jnp.bfloat16)
        return carry

    lax.fori_loop(0, half, time_close, 0)

    for way in range(2):
        give(way).wait_send()
        for a in range(2):
            halo(way, a).wait_send()
    for piece in range(pieces):
        for r in steps:
            other = lax.rem(pos + r, n)
            for a in range(4):
                fwd(a, piece, other, pos).wait_send()
            for a in range(3):
                backward(a, piece, other, pos).wait_send()
    for piece in range(pieces):
        for a in range(3):
            self_out(a, piece).wait()
            for r in steps:
                source = lax.rem(pos + r, n)
                backward(a, piece, source, source).wait_recv()


def put_out(*refs):
    count = (len(refs) - 1) // 2
    copies = [
        pltpu.make_async_copy(refs[a], refs[count + a], refs[-1].at[a]) for a in range(count)
    ]
    for copy in copies:
        copy.start()
    for copy in copies:
        copy.wait()


def solution(mesh):
    n, segs = mesh.shape["pos"], mesh.shape["seg"]

    def on_device(*args):
        frames, heads, rows, width = args[0].shape
        half = heads // 2
        items = frames * half // n
        limit = max(1, items // PARTS)
        chunk = max(c for c in range(1, limit + 1) if items % c == 0 and half % c == 0)
        pieces = items // chunk
        low = jnp.bfloat16
        block = (half, rows, width)
        any_spec = pl.BlockSpec(memory_space=pl.ANY)
        smem_spec = pl.BlockSpec(memory_space=pltpu.SMEM)
        dma = pltpu.SemaphoreType.DMA
        out = jax.ShapeDtypeStruct(args[0].shape, low)
        vmem_out = pltpu.VMEM(args[0].shape, low)
        vmem_spec = pl.BlockSpec(memory_space=pltpu.VMEM)
        grads = pl.pallas_call(
            functools.partial(kernel, n, segs, chunk),
            out_shape=(vmem_out,) * 3,
            in_specs=[any_spec] * 4 + [smem_spec] * 3,
            out_specs=(vmem_spec,) * 3,
            scratch_shapes=[
                pltpu.VMEM((4, items, n * rows, width), low),
                pltpu.VMEM((3, items, n * rows, width), low),
                pltpu.VMEM((items, n * rows, n * rows), jnp.float32),
                pltpu.VMEM((items, n * rows, n * rows), low),
                pltpu.VMEM((2, frames) + block, low),
                pltpu.VMEM((2, frames + 2 * WMAX) + block, low),
                pltpu.VMEM((2, 2, WMAX) + block, low),
                pltpu.VMEM((2, 2, WMAX) + block, low),
                pltpu.VMEM((2, frames) + block, jnp.float32),
                dma((4, pieces, n)),
                dma((4, pieces, n)),
                dma((3, pieces, n)),
                dma((3, pieces, n)),
                dma((2, 2)),
                dma((2, 2)),
                dma((2,)),
                dma((2,)),
                dma((7, pieces)),
                dma((4,)),
            ],
            compiler_params=pltpu.CompilerParams(collective_id=0, has_side_effects=True),
        )(*args)
        return pl.pallas_call(
            put_out,
            out_shape=(out, out, out),
            in_specs=[vmem_spec] * 3,
            out_specs=(any_spec,) * 3,
            scratch_shapes=[dma((3,))],
        )(*(pltpu.with_memory_space_constraint(x, pltpu.VMEM) for x in grads))

    heads_spec = P("seg", None, "pos", None)
    return jax.shard_map(
        on_device,
        mesh=mesh,
        in_specs=(heads_spec,) * 4 + (P(),) * 3,
        out_specs=(heads_spec,) * 3,
        check_vma=False,
    )
```

profile of v0, /device:TPU:0, one launch (start us, length us, event | category | flops | bytes accessed | tf_op | source)
XLA Modules:
  0.0 38.8 jit_solution(16715309914695412613)
XLA Ops:
  0.6 37.2 %shard_map.94 = (bf16[4,12,32,128]{3,2,1,0:T(8,128)(2,1)S(1)}, bf16[4,12,32,128]{3,2,1,0:T(8,128)(2,1)S(1)}, bf16[4,12,32,128]{3,2,1,0:T(8,128)(2,1)S(1)}) custom-call(bf16[4,12,32,128]{3,2,1,0:T(8,128)(2,1)} %q_ref.1, bf16[4,12,32,128]{3,2,1,0:T(8,128)(2,1)} %k_ref.1, bf16[4,12,32,128]{3,2,1,0:T(8,128)(2,1)} %v_ref.1, bf16[4,12,32,128]{3,2,1,0:T(8,128)(2,1)} %g_ref.1, ...), custom_call_target="tpu_custom_call" | custom-call | tf_op jit(solution)/shard_map/pallas_call | solution.py:366
  37.8 1.0 %shard_map.95 = (bf16[4,12,32,128]{3,2,1,0:T(8,128)(2,1)}, bf16[4,12,32,128]{3,2,1,0:T(8,128)(2,1)}, bf16[4,12,32,128]{3,2,1,0:T(8,128)(2,1)}) custom-call(bf16[4,12,32,128]{3,2,1,0:T(8,128)(2,1)S(1)} %get-tuple-element.6.refs_0_, bf16[4,12,32,128]{3,2,1,0:T(8,128)(2,1)S(1)} %get-tuple-element.7.refs_1_, bf16[4,12,32,128]{3,2,1,0:T(8,128)(2,1)S(1)} %get-tuple-element.8.refs_2_), custom_call_target="tpu_custom_call" | custom-call | tf_op jit(solution)/shard_map/pallas_call | solution.py:394
where the time goes:
time: 39 us; the launch traced here: 38.8 us
  Pallas kernels  38.2 us (98%)
  between operations  0.64 us (2%)
    pallas_call x1, Pallas kernels, on_device(): pl.pallas_call(functools.partial(kernel, n, segs, chunk), out_shape=(vmem...  37.2 us
    pallas_call x1, Pallas kernels, on_device(): pl.pallas_call(put_out, out_shape=(out, out, out), in_specs=[vmem_spec] *...  1.03 us

commit v1 on v0

v1 whole, which is shorter than its diff:
```python
import functools
import math

import jax
import jax.numpy as jnp
from jax import lax
from jax.experimental import pallas as pl
from jax.experimental.pallas import tpu as pltpu
from jax.sharding import PartitionSpec as P

WMAX = 2
MESH = pl.DeviceIdType.MESH
CHUNK = 3
AHEAD = 2
FAR = -1e30


def matmul(left, right, dims):
    return lax.dot_general(left, right, (dims, ((), ())), preferred_element_type=jnp.float32)


def kernel(
    n,
    segs,
    chunk,
    q_ref,
    k_ref,
    v_ref,
    g_ref,
    len_ref,
    res_ref,
    win_ref,
    oq_ref,
    ok_ref,
    ov_ref,
    qg,
    kv,
    powers_of,
    slopes,
    mine,
    theirs,
    part,
    cast,
    given,
    back,
    tqg,
    ekv,
    edge,
    redge,
    own,
    up_s,
    up_r,
    over_s,
    over_r,
    stat_s,
    stat_r,
    part_s,
    part_r,
    down_s,
    down_r,
    halo_s,
    halo_r,
    ret_s,
    ret_r,
    in_s,
    out_s,
    time_s,
):
    frames, heads, rows, width = q_ref.shape
    half = heads // 2
    pieces = frames * half // chunk
    groups = half // chunk
    m = n // 2
    keys_held = m * rows
    positions = n * rows
    inv_root = 1.0 / math.sqrt(width)
    ins = (q_ref, g_ref, k_ref, v_ref)
    outs = (oq_ref, ok_ref, ov_ref)
    seg = lax.axis_index("seg")
    pos = lax.axis_index("pos")
    right = lax.rem(seg + 1, segs)
    left = lax.rem(seg + segs - 1, segs)
    side = lax.div(pos, m)
    spot = pos - side * m
    hub_spot = (m - 1) * (1 - side)
    hub = side * m + hub_spot
    peer = n - 1 - hub
    peer_spot = (m - 1) * side
    is_hub = pos == hub

    def rows_of(p):
        return pl.ds(pl.multiple_of(p * rows, rows), rows)

    def half_of(p):
        return pl.ds(pl.multiple_of(p * keys_held, keys_held), keys_held)

    def block(ref, piece):
        return ref.at[piece // groups, pl.ds(piece % groups * chunk, chunk)]

    def span(piece):
        return pl.ds(piece * chunk, chunk)

    def slot(a, piece, spot):
        if a < 2:
            return qg.at[a, span(piece), rows_of(side * m + spot)]
        return kv.at[a - 2, span(piece), rows_of(spot)]

    def remote(src, dst, send, recv, dest):
        return pltpu.make_async_remote_copy(
            src_ref=src,
            dst_ref=dst,
            send_sem=send,
            recv_sem=recv,
            device_id=(seg, dest),
            device_id_type=MESH,
        )

    def up(a, piece, spot):
        return remote(
            block(ins[a], piece),
            slot(a, piece, spot),
            up_s.at[a, piece],
            up_r.at[a, piece, spot],
            hub,
        )

    def over(a, piece, spot, where, source):
        return remote(
            source,
            qg.at[a, span(piece), rows_of(where * m + spot)],
            over_s.at[a, piece, spot],
            over_r.at[a, piece, spot],
            peer,
        )

    def over_own(a, piece):
        return over(a, piece, hub_spot, side, block(ins[a], piece))

    def over_next(a, piece, spot):
        return over(a, piece, spot, side, slot(a, piece, spot))

    def over_in(a, piece, spot):
        return over(a, piece, spot, 1 - side, block(ins[a], piece))

    def stat(piece):
        return remote(mine.at[piece], theirs.at[piece], stat_s.at[piece], stat_r.at[piece], peer)

    def cross(piece):
        return remote(
            cast.at[span(piece), half_of(1 - side)],
            given.at[span(piece)],
            part_s.at[piece],
            part_r.at[piece],
            peer,
        )

    def down(a, piece, spot, dest):
        return remote(
            back.at[a, span(piece), rows_of(spot)],
            block(outs[a], piece),
            down_s.at[a, piece, spot],
            down_r.at[a, piece],
            dest,
        )

    def self_in(a, piece):
        return pltpu.make_async_copy(
            block(ins[a], piece), slot(a, piece, hub_spot), in_s.at[a, piece]
        )

    def self_out(a, piece):
        return pltpu.make_async_copy(
            back.at[a, span(piece), rows_of(hub_spot)], block(outs[a], piece), out_s.at[a, piece]
        )

    def time_half(ref, first, count):
        return ref.at[pl.ds(first, count), pl.ds(half, half)]

    def halo(way, a):
        source = (k_ref, v_ref)[a]
        if way == 0:
            src, dst, dest = time_half(source, frames - WMAX, WMAX), 0, right
        else:
            src, dst, dest = time_half(source, 0, WMAX), frames + WMAX, left
        return pltpu.make_async_remote_copy(
            src_ref=src,
            dst_ref=ekv.at[a, pl.ds(dst, WMAX)],
            send_sem=halo_s.at[way, a],
            recv_sem=halo_r.at[way, a],
            device_id=(dest, pos),
            device_id_type=MESH,
        )

    def give(way):
        return pltpu.make_async_remote_copy(
            src_ref=edge.at[way],
            dst_ref=redge.at[way],
            send_sem=ret_s.at[way],
            recv_sem=ret_r.at[way],
            device_id=((left, right)[way], pos),
            device_id_type=MESH,
        )

    time_in = [
        pltpu.make_async_copy(time_half(q_ref, 0, frames), tqg.at[0], time_s.at[0]),
        pltpu.make_async_copy(time_half(g_ref, 0, frames), tqg.at[1], time_s.at[1]),
        pltpu.make_async_copy(
            time_half(k_ref, 0, frames), ekv.at[0, pl.ds(WMAX, frames)], time_s.at[2]
        ),
        pltpu.make_async_copy(
            time_half(v_ref, 0, frames), ekv.at[1, pl.ds(WMAX, frames)], time_s.at[3]
        ),
    ]

    others = [lax.rem(hub_spot + r, m) for r in range(1, m)]
    peers_others = [lax.rem(peer_spot + r, m) for r in range(1, m)]
    barrier = pltpu.get_barrier_semaphore()

    def greet(where, dest):
        pl.semaphore_signal(barrier, inc=1, device_id=(where, dest), device_id_type=MESH)

    for near in (left, right):
        greet(near, pos)

    @pl.when(is_hub)
    def _():
        greet(seg, peer)
        for spot in others:
            greet(seg, side * m + spot)
        for piece in range(pieces):
            for a in range(4):
                self_in(a, piece).start()

    @pl.when(jnp.logical_not(is_hub))
    def _():
        greet(seg, hub)

    for copy in time_in:
        copy.start()

    @pl.when(is_hub)
    def _():
        pl.semaphore_wait(barrier, m + 2)
        for piece in range(min(2 * AHEAD, pieces)):
            for a in range(2):
                over_own(a, piece).start()

    @pl.when(jnp.logical_not(is_hub))
    def _():
        pl.semaphore_wait(barrier, 3)
        for piece in range(pieces):
            for a in range(4):
                up(a, piece, spot).start()

    for way in range(2):
        for a in range(2):
            halo(way, a).start()

    ext = frames + 2 * WMAX
    base = seg * frames
    zero = jnp.int32(0)

    def clip_step(c, carry):
        start, owners, live, wins = carry
        end = start + len_ref[c]
        owners = tuple(
            o + jnp.where(end <= base + (x - WMAX), 1, 0) for x, o in enumerate(owners)
        )
        inside = [(start <= base + x) & (base + x < end) for x in range(frames)]
        live = tuple(jnp.where(i, res_ref[c], o) for i, o in zip(inside, live))
        wins = tuple(jnp.where(i, win_ref[c], o) for i, o in zip(inside, wins))
        return end, owners, live, wins

    _, owners, live, wins = lax.fori_loop(
        0, len_ref.shape[0], clip_step, (zero, (zero,) * ext, (zero,) * frames, (zero,) * frames)
    )
    owners = [jnp.where(base + (x - WMAX) < 0, -1, o) for x, o in enumerate(owners)]
    bias = [
        [
            jnp.where(
                (owners[i + o] == owners[i + WMAX]) & (wins[i] >= abs(o - WMAX)), 0.0, -jnp.inf
            ).astype(jnp.float32)
            for o in range(2 * WMAX + 1)
        ]
        for i in range(frames)
    ]

    def time_head(h, carry):
        row = lax.broadcasted_iota(jnp.int32, (rows, 1), 0) + pos * rows
        keys = [ekv[0, j, h].astype(jnp.float32) for j in range(ext)]
        values = [ekv[1, j, h].astype(jnp.float32) for j in range(ext)]
        key_sum = [None] * ext
        value_sum = [None] * ext
        for i in range(frames):
            query = tqg[0, i, h].astype(jnp.float32)
            grad = tqg[1, i, h].astype(jnp.float32)
            offsets = range(2 * WMAX + 1)
            scores = [
                jnp.sum(query * keys[i + o], axis=1, keepdims=True) * inv_root + bias[i][o]
                for o in offsets
            ]
            dweights = [jnp.sum(grad * values[i + o], axis=1, keepdims=True) for o in offsets]
            top = functools.reduce(jnp.maximum, scores)
            powers = [jnp.exp(s - top) for s in scores]
            scale = jnp.where(row < live[i], 1.0 / sum(powers[1:], powers[0]), 0.0)
            weights = [p * scale for p in powers]
            low = [w.astype(jnp.bfloat16).astype(jnp.float32) for w in weights]
            dots = [w * d for w, d in zip(low, dweights)]
            row_dot = sum(dots[1:], dots[0])
            dscores = [
                (w * (d - row_dot)).astype(jnp.bfloat16).astype(jnp.float32)
                for w, d in zip(weights, dweights)
            ]
            terms = [dscores[o] * keys[i + o] for o in offsets]
            oq_ref[i, half + h] = (sum(terms[1:], terms[0]) * inv_root).astype(jnp.bfloat16)
            for o in offsets:
                j = i + o
                key_term = dscores[o] * query
                value_term = low[o] * grad
                key_sum[j] = key_term if key_sum[j] is None else key_sum[j] + key_term
                value_sum[j] = value_term if value_sum[j] is None else value_sum[j] + value_term
        for a, sums in enumerate((key_sum, value_sum)):
            factor = inv_root if a == 0 else 1.0
            for j in range(WMAX):
                edge[0, a, j, h] = (sums[j] * factor).astype(jnp.bfloat16)
                edge[1, a, j, h] = (sums[frames + WMAX + j] * factor).astype(jnp.bfloat16)
            for i in range(frames):
                own[a, i, h] = sums[WMAX + i] * factor
        return carry

    def time_close(h, carry):
        for a in range(2):
            for i in range(frames):
                total = own[a, i, h]
                if i < WMAX:
                    total = total + redge[1, a, i, h].astype(jnp.float32)
                if i >= frames - WMAX:
                    total = total + redge[0, a, i - (frames - WMAX), h].astype(jnp.float32)
                outs[1 + a][i, half + h] = total.astype(jnp.bfloat16)
        return carry

    def time_begin():
        for copy in time_in:
            copy.wait()
        for way in range(2):
            for a in range(2):
                halo(way, a).wait_recv()

    def time_send():
        for way in range(2):
            give(way).start()

    def time_end():
        for way in range(2):
            give(way).wait_recv()
        lax.fori_loop(0, half, time_close, 0)

    def pass_on(piece):
        for a in range(2):
            for spot in others:
                up(a, piece, spot).wait_recv()
                over_next(a, piece, spot).start()

    def score(piece):
        for a in range(4):
            self_in(a, piece).wait()
            if a >= 2:
                for spot in others:
                    up(a, piece, spot).wait_recv()
        for a in range(2):
            over_in(a, piece, peer_spot).wait_recv()
            for spot in peers_others:
                over_in(a, piece, spot).wait_recv()
        limit = live[piece // groups]
        key = lax.broadcasted_iota(jnp.int32, (keys_held, 1), 0) + side * keys_held
        for i in range(chunk):
            t = piece * chunk + i
            scores = matmul(kv[0, t], qg[0, t], ((1,), (1,))) * inv_root
            scores = jnp.where(key < limit, scores, FAR)
            top = jnp.max(scores, axis=0, keepdims=True)
            powers = jnp.exp(scores - top)
            dweights = matmul(kv[1, t], qg[1, t], ((1,), (1,)))
            powers_of[t] = powers
            slopes[t] = dweights
            mine[piece, pl.ds(i, 1)] = top
            mine[piece, pl.ds(chunk + i, 1)] = jnp.sum(powers, axis=0, keepdims=True)
            mine[piece, pl.ds(2 * chunk + i, 1)] = jnp.sum(powers * dweights, axis=0, keepdims=True)
        stat(piece).start()

    def solve(piece):
        stat(piece).wait_recv()
        limit = live[piece // groups]
        query = lax.broadcasted_iota(jnp.int32, (1, positions), 1)
        for i in range(chunk):
            t = piece * chunk + i
            top, total, dot = (mine[piece, pl.ds(k * chunk + i, 1)] for k in range(3))
            top_in, total_in, dot_in = (theirs[piece, pl.ds(k * chunk + i, 1)] for k in range(3))
            high = jnp.maximum(top, top_in)
            low_in = jnp.exp(top_in - high)
            low_own = jnp.exp(top - high)
            inverse = 1.0 / (total * low_own + total_in * low_in)
            row_dot = (dot * low_own + dot_in * low_in) * inverse
            weights = powers_of[t] * jnp.where(query < limit, low_own * inverse, 0.0)
            dscores = (weights * (slopes[t] - row_dot)).astype(jnp.bfloat16)
            query_part = matmul(dscores, kv[0, t], ((0,), (0,))) * inv_root
            part[t] = query_part
            cast[t] = query_part.astype(jnp.bfloat16)
            key_part = matmul(dscores, qg[0, t], ((1,), (0,))) * inv_root
            back[1, t] = key_part.astype(jnp.bfloat16)
            value_part = matmul(weights.astype(jnp.bfloat16), qg[1, t], ((1,), (0,)))
            back[2, t] = value_part.astype(jnp.bfloat16)
        cross(piece).start()
        for a in (1, 2):
            hand(a, piece)

    def hand(a, piece):
        for spot in others:
            down(a, piece, spot, side * m + spot).start()
        self_out(a, piece).start()

    def settle(piece):
        cross(piece).wait_recv()
        for i in range(chunk):
            t = piece * chunk + i
            total = part[t, half_of(side)] + given[t].astype(jnp.float32)
            back[0, t] = total.astype(jnp.bfloat16)
        hand(0, piece)

    @pl.when(is_hub)
    def _():
        for piece in range(min(AHEAD, pieces)):
            pass_on(piece)
        for piece in range(2 * AHEAD, min(3 * AHEAD, pieces)):
            for a in range(2):
                over_own(a, piece).start()
        busy = max(1, pieces - 2)
        for piece in range(pieces):
            score(piece)
            if piece + AHEAD < pieces:
                pass_on(piece + AHEAD)
            if piece + 3 * AHEAD < pieces:
                for a in range(2):
                    over_own(a, piece + 3 * AHEAD).start()
            if piece == 0:
                time_begin()
            if piece < busy:
                lax.fori_loop(piece * half // busy, (piece + 1) * half // busy, time_head, 0)
            if piece == busy - 1:
                time_send()
            if piece == pieces - 1:
                time_end()
            solve(piece)
            if piece > 0:
                settle(piece - 1)
        settle(pieces - 1)

        for piece in range(pieces):
            stat(piece).wait_send()
            cross(piece).wait_send()
            for a in range(2):
                over_own(a, piece).wait_send()
                for spot in others:
                    over_next(a, piece, spot).wait_send()
            for a in range(3):
                self_out(a, piece).wait()
                for spot in others:
                    down(a, piece, spot, side * m + spot).wait_send()

    @pl.when(jnp.logical_not(is_hub))
    def _():
        time_begin()
        lax.fori_loop(0, half, time_head, 0)
        time_send()
        time_end()
        for piece in range(pieces):
            for a in range(4):
                up(a, piece, spot).wait_send()
            for a in range(3):
                down(a, piece, spot, hub).wait_recv()

    for way in range(2):
        give(way).wait_send()
        for a in range(2):
            halo(way, a).wait_send()


def put_out(*refs):
    count = (len(refs) - 1) // 2
    copies = [
        pltpu.make_async_copy(refs[a], refs[count + a], refs[-1].at[a]) for a in range(count)
    ]
    for copy in copies:
        copy.start()
    for copy in copies:
        copy.wait()


def solution(mesh):
    n, segs = mesh.shape["pos"], mesh.shape["seg"]

    def on_device(*args):
        frames, heads, rows, width = args[0].shape
        half = heads // 2
        items = frames * half
        chunk = max(c for c in range(1, CHUNK + 1) if half % c == 0)
        pieces = items // chunk
        m = n // 2
        low = jnp.bfloat16
        block = (half, rows, width)
        any_spec = pl.BlockSpec(memory_space=pl.ANY)
        smem_spec = pl.BlockSpec(memory_space=pltpu.SMEM)
        dma = pltpu.SemaphoreType.DMA
        out = jax.ShapeDtypeStruct(args[0].shape, low)
        vmem_out = pltpu.VMEM(args[0].shape, low)
        vmem_spec = pl.BlockSpec(memory_space=pltpu.VMEM)
        grads = pl.pallas_call(
            functools.partial(kernel, n, segs, chunk),
            out_shape=(vmem_out,) * 3,
            in_specs=[any_spec] * 4 + [smem_spec] * 3,
            out_specs=(vmem_spec,) * 3,
            scratch_shapes=[
                pltpu.VMEM((2, items, n * rows, width), low),
                pltpu.VMEM((2, items, m * rows, width), low),
                pltpu.VMEM((items, m * rows, n * rows), jnp.float32),
                pltpu.VMEM((items, m * rows, n * rows), jnp.float32),
                pltpu.VMEM((pieces, 3 * chunk, n * rows), jnp.float32),
                pltpu.VMEM((pieces, 3 * chunk, n * rows), jnp.float32),
                pltpu.VMEM((items, n * rows, width), jnp.float32),
                pltpu.VMEM((items, n * rows, width), low),
                pltpu.VMEM((items, m * rows, width), low),
                pltpu.VMEM((3, items, m * rows, width), low),
                pltpu.VMEM((2, frames) + block, low),
                pltpu.VMEM((2, frames + 2 * WMAX) + block, low),
                pltpu.VMEM((2, 2, WMAX) + block, low),
                pltpu.VMEM((2, 2, WMAX) + block, low),
                pltpu.VMEM((2, frames) + block, jnp.float32),
                dma((4, pieces)),
                dma((4, pieces, m)),
                dma((2, pieces, m)),
                dma((2, pieces, m)),
                dma((pieces,)),
                dma((pieces,)),
                dma((pieces,)),
                dma((pieces,)),
                dma((3, pieces, m)),
                dma((3, pieces)),
                dma((2, 2)),
                dma((2, 2)),
                dma((2,)),
                dma((2,)),
                dma((4, pieces)),
                dma((3, pieces)),
                dma((4,)),
            ],
            compiler_params=pltpu.CompilerParams(collective_id=0, has_side_effects=True),
        )(*args)
        return pl.pallas_call(
            put_out,
            out_shape=(out, out, out),
            in_specs=[vmem_spec] * 3,
            out_specs=(any_spec,) * 3,
            scratch_shapes=[dma((3,))],
        )(*(pltpu.with_memory_space_constraint(x, pltpu.VMEM) for x in grads))

    heads_spec = P("seg", None, "pos", None)
    return jax.shard_map(
        on_device,
        mesh=mesh,
        in_specs=(heads_spec,) * 4 + (P(),) * 3,
        out_specs=(heads_spec,) * 3,
        check_vma=False,
    )
```

time: 39 us -> 52.6 us (1.35)
  Pallas kernels: 38.2 us -> 51.8 us
    pallas_call x1, Pallas kernels: 37.2 us -> 50.7 us  [on_device(): pl.pallas_call(functools.partial(kernel, n, segs, chunk), out_shape=(vmem...]
where the time goes in v1:
time: 52.6 us; the launch traced here: 52.4 us
  Pallas kernels  51.8 us (98%)
  between operations  0.64 us (1%)
    pallas_call x1, Pallas kernels, on_device(): pl.pallas_call(functools.partial(kernel, n, segs, chunk), out_shape=(vmem...  50.7 us

profile of v1, /device:TPU:0, one launch (start us, length us, event | category | flops | bytes accessed | tf_op | source)
XLA Modules:
  0.0 52.4 jit_solution(17984697619954173681)
XLA Ops:
  0.6 50.7 %shard_map.94 = (bf16[4,12,32,128]{3,2,1,0:T(8,128)(2,1)S(1)}, bf16[4,12,32,128]{3,2,1,0:T(8,128)(2,1)S(1)}, bf16[4,12,32,128]{3,2,1,0:T(8,128)(2,1)S(1)}) custom-call(bf16[4,12,32,128]{3,2,1,0:T(8,128)(2,1)} %q_ref.1, bf16[4,12,32,128]{3,2,1,0:T(8,128)(2,1)} %k_ref.1, bf16[4,12,32,128]{3,2,1,0:T(8,128)(2,1)} %v_ref.1, bf16[4,12,32,128]{3,2,1,0:T(8,128)(2,1)} %g_ref.1, ...), custom_call_target="tpu_custom_call" | custom-call | tf_op jit(solution)/shard_map/pallas_call | solution.py:516
  51.4 1.0 %shard_map.95 = (bf16[4,12,32,128]{3,2,1,0:T(8,128)(2,1)}, bf16[4,12,32,128]{3,2,1,0:T(8,128)(2,1)}, bf16[4,12,32,128]{3,2,1,0:T(8,128)(2,1)}) custom-call(bf16[4,12,32,128]{3,2,1,0:T(8,128)(2,1)S(1)} %get-tuple-element.6.refs_0_, bf16[4,12,32,128]{3,2,1,0:T(8,128)(2,1)S(1)} %get-tuple-element.7.refs_1_, bf16[4,12,32,128]{3,2,1,0:T(8,128)(2,1)S(1)} %get-tuple-element.8.refs_2_), custom_call_target="tpu_custom_call" | custom-call | tf_op jit(solution)/shard_map/pallas_call | solution.py:557

commit v2 on v0

--- a/solution.py
+++ b/solution.py
@@ -50,6 +50,8 @@
     ret_r,
     self_s,
     time_s,
+    known_s,
+    beside_s,
 ):
     frames, heads, rows, width = q_ref.shape
     half = heads // 2
@@ -63,7 +65,17 @@
     pos = lax.axis_index("pos")
     right = lax.rem(seg + 1, segs)
     left = lax.rem(seg + segs - 1, segs)
-    steps = sorted(range(1, n), key=lambda r: abs(r - n // 2))
+    middle = n // 2
+    upper = pos >= middle
+    steps = range(1, n)
+    targets = [
+        jnp.where(
+            upper,
+            jnp.where(i < pos, i, i + 1),
+            jnp.where(n - 1 - i > pos, n - 1 - i, n - 2 - i),
+        )
+        for i in range(n - 1)
+    ]
 
     def rows_of(p):
         return pl.ds(pl.multiple_of(p * rows, rows), rows)
@@ -146,27 +158,106 @@
     ]
 
     barrier = pltpu.get_barrier_semaphore()
-    for r in steps:
-        pl.semaphore_signal(
-            barrier, inc=1, device_id=(seg, lax.rem(pos + r, n)), device_id_type=MESH
-        )
-    for near in (left, right):
-        pl.semaphore_signal(barrier, inc=1, device_id=(near, pos), device_id_type=MESH)
+    even = lax.rem(seg, 2) == 0
+    inward = jnp.where(upper, pos - 1, pos + 1)
+    outward = jnp.where(upper, pos + 1, pos - 1)
+    centre = (pos == middle - 1) | (pos == middle)
+    rim = (pos == 0) | (pos == n - 1)
+
+    def signal(sem, where, dest):
+        pl.semaphore_signal(sem, inc=1, device_id=(where, dest), device_id_type=MESH)
+
+    @pl.when(centre)
+    def _():
+        signal(barrier, seg, inward)
+
+    @pl.when(jnp.logical_not(rim))
+    def _():
+        signal(barrier, seg, outward)
+
+    @pl.when(even)
+    def _():
+        for beside in (left, right):
+            signal(barrier, beside, pos)
+
     for copy in time_in:
         copy.start()
     for piece in range(pieces):
         for a in range(4):
             self_in(a, piece).start()
-    pl.semaphore_wait(barrier, n + 1)
-
-    for piece in range(pieces):
-        for a in (0, 1, 3, 2):
-            for r in steps:
-                fwd(a, piece, lax.rem(pos + r, n), pos).start()
-        if piece == 0:
-            for way in range(2):
-                for a in range(2):
-                    halo(way, a).start()
+
+    @pl.when(even)
+    def _():
+        pl.semaphore_wait(barrier, 1)
+
+    @pl.when(jnp.logical_not(even))
+    def _():
+        pl.semaphore_wait(barrier, 3)
+
+    def push(arrays, dest):
+        for piece in range(pieces):
+            for a in arrays:
+                fwd(a, piece, dest, pos).start()
+
+    push((0, 1, 3), inward)
+
+    @pl.when(jnp.logical_not(centre))
+    def _():
+        signal(known_s.at[jnp.where(upper, 1, 0), 1], seg, inward)
+
+    @pl.when(jnp.logical_not(even))
+    def _():
+        signal(beside_s.at[1], left, pos)
+        signal(beside_s.at[0], right, pos)
+
+    @pl.when(jnp.logical_not(rim))
+    def _():
+        pl.semaphore_wait(known_s.at[jnp.where(upper, 1, 0), 1], 1)
+        push((0, 1), outward)
+
+    def present(way, reach):
+        return pos >= reach if way == 0 else pos + reach < n
+
+    def relay(way, reach):
+        if reach + 1 < n:
+
+            @pl.when(present(1 - way, 1))
+            def _():
+                signal(known_s.at[way, reach + 1], seg, pos + 1 - 2 * way)
+
+    for way in range(2):
+
+        @pl.when(present(way, 1))
+        def _():
+            relay(way, 1)
+
+    @pl.when(even)
+    def _():
+        for way in range(2):
+            pl.semaphore_wait(beside_s.at[way], 1)
+
+    for way in range(2):
+        for a in range(2):
+            halo(way, a).start()
+
+    for reach in range(2, n):
+        for way in range(2):
+
+            @pl.when(present(way, reach))
+            def _():
+                pl.semaphore_wait(known_s.at[way, reach], 1)
+                relay(way, reach)
+                push((0, 1), pos + (2 * way - 1) * reach)
+
+    for a in (3, 2):
+        for dest in targets:
+            if a == 2:
+                push((a,), dest)
+            else:
+
+                @pl.when(dest != inward)
+                def _():
+                    push((a,), dest)
 
     ext = frames + 2 * WMAX
     base = seg * frames
@@ -257,8 +348,8 @@
             fwd(a, piece, source, source).wait_recv()
 
     def send(a, piece):
-        for r in steps:
-            backward(a, piece, lax.rem(pos + r, n), pos).start()
+        for dest in targets:
+            backward(a, piece, dest, pos).start()
         self_out(a, piece).start()
 
     for piece in range(pieces):
@@ -388,6 +479,8 @@
                 dma((2,)),
                 dma((7, pieces)),
                 dma((4,)),
+                pltpu.SemaphoreType.REGULAR((2, n)),
+                pltpu.SemaphoreType.REGULAR((2,)),
             ],
             compiler_params=pltpu.CompilerParams(collective_id=0, has_side_effects=True),
         )(*args)

time: 39 us -> 37.9 us (0.972)
  Pallas kernels: 38.2 us -> 36.8 us
    pallas_call x1, Pallas kernels: 37.2 us -> 35.8 us  [on_device(): pl.pallas_call(functools.partial(kernel, n, segs, chunk), out_shape=(vmem...]
where the time goes in v2:
time: 37.9 us; the launch traced here: 37.5 us
  Pallas kernels  36.8 us (97%)
  between operations  0.64 us (2%)
    pallas_call x1, Pallas kernels, on_device(): pl.pallas_call(functools.partial(kernel, n, segs, chunk), out_shape=(vmem...  35.8 us
    pallas_call x1, Pallas kernels, on_device(): pl.pallas_call(put_out, out_shape=(out, out, out), in_specs=[vmem_spec] *...  1.03 us

profile of v2, /device:TPU:0, one launch (start us, length us, event | category | flops | bytes accessed | tf_op | source)
XLA Modules:
  0.0 37.5 jit_solution(444203058977174938)
XLA Ops:
  0.6 35.8 %shard_map.94 = (bf16[4,12,32,128]{3,2,1,0:T(8,128)(2,1)S(1)}, bf16[4,12,32,128]{3,2,1,0:T(8,128)(2,1)S(1)}, bf16[4,12,32,128]{3,2,1,0:T(8,128)(2,1)S(1)}) custom-call(bf16[4,12,32,128]{3,2,1,0:T(8,128)(2,1)} %q_ref.1, bf16[4,12,32,128]{3,2,1,0:T(8,128)(2,1)} %k_ref.1, bf16[4,12,32,128]{3,2,1,0:T(8,128)(2,1)} %v_ref.1, bf16[4,12,32,128]{3,2,1,0:T(8,128)(2,1)} %g_ref.1, ...), custom_call_target="tpu_custom_call" | custom-call | tf_op jit(solution)/shard_map/pallas_call | solution.py:457
  36.4 1.0 %shard_map.95 = (bf16[4,12,32,128]{3,2,1,0:T(8,128)(2,1)}, bf16[4,12,32,128]{3,2,1,0:T(8,128)(2,1)}, bf16[4,12,32,128]{3,2,1,0:T(8,128)(2,1)}) custom-call(bf16[4,12,32,128]{3,2,1,0:T(8,128)(2,1)S(1)} %get-tuple-element.6.refs_0_, bf16[4,12,32,128]{3,2,1,0:T(8,128)(2,1)S(1)} %get-tuple-element.7.refs_1_, bf16[4,12,32,128]{3,2,1,0:T(8,128)(2,1)S(1)} %get-tuple-element.8.refs_2_), custom_call_target="tpu_custom_call" | custom-call | tf_op jit(solution)/shard_map/pallas_call | solution.py:487
